TPU v7x, 512 devices: a whole 4x4x16 slice. The times are simulated.
512 devices in a mesh: rows: 128 (over x, z, core), grp: 4 (over y).
Axes of the slice: x: 4, y: 4, z: 16, core: 2. Of those that a mesh axis runs over, the one named last changes fastest.
Arguments:
- a_blocks: float32 [4096, 7, 128, 128], P(('rows', 'grp')), may hold values from -0.5 to 0.5
- neighbours: int32 [4096, 7], P(('rows', 'grp')), may hold values from 0 to 4095, as said below
- neighbour_count: int32 [4096], P(('rows', 'grp')), may hold values from 1 to 7
- p_blocks: float32 [4096, 2, 128, 128], P(('rows', 'grp')), may hold values from -1 to 1
- p_columns: int32 [4096, 2], P(('rows', 'grp')), may hold values from 0 to 511, as said below
- p_count: int32 [4096], P(('rows', 'grp')), may hold values from 1 to 2
- coarse_slot: int32 [512], replicated, may hold values from 0 to 3, as said below
- coarse_pattern: int32 [512, 4], replicated, may hold values from 0 to 511, as said below
Outputs:
- coarse_op: float32 [512, 4, 128, 128], P(('rows', 'grp'))
Inputs may be any that keep to these rules, and one draw needn't show every extreme that they name: neighbours[e,0] = e; every neighbour of an element of the slab of 32 elements that holds it lies in that slab or within 8 elements before or after it. The elements of slab q form aggregates q * 4 to (q + 1) * 4 - 1, eight elements each; p_columns[e,0] is the aggregate of e, and every slot names an aggregate of the element's slab or of a slab beside it. `coarse_slot`: within each slab the aggregates take each position 0 to 3 once. coarse_pattern[c,0] = c; every column is an aggregate of c's slab or of a slab beside it; columns may repeat.
All inputs are finite; a program needn't handle non-finite values.
Results may differ from a plain program's by a relative error of at most 0.0003.
Values sent between devices are 32-bit elements; how exact they have to be, the bound alone decides.
A program may use at most 64 MiB of HBM per device.

v0:
```python
import jax
import jax.numpy as jnp
from jax import lax
from jax.sharding import PartitionSpec as P

HIGH = lax.Precision.HIGHEST


def shifted(value, axis, steps):
    count = lax.axis_size(axis)
    initial, last = (max(0, -steps), min(count, count - steps))
    return lax.ppermute(value, axis, [(source, source + steps) for source in range(initial, last)])


def per_device(
    a_blocks, neighbours, neighbour_count, p_blocks, p_columns, p_count, coarse_slot, coarse_pattern
):
    groups = lax.axis_size("grp")
    e_local = a_blocks.shape[0]
    slab_len = groups * e_local
    agg_slab = slab_len // 8
    n_slot = a_blocks.shape[1]
    p_slot = p_blocks.shape[1]
    row_index = lax.axis_index("rows")
    slab_p, slab_cols, slab_count = (
        lax.all_gather(p_blocks, "grp", axis=0, tiled=True),
        lax.all_gather(p_columns, "grp", axis=0, tiled=True),
        lax.all_gather(p_count, "grp", axis=0, tiled=True),
    )
    prev_p, prev_cols, prev_count = shifted(
        (
            slab_p[slab_len - e_local :],
            slab_cols[slab_len - e_local :],
            slab_count[slab_len - e_local :],
        ),
        "rows",
        1,
    )
    next_p, next_cols, next_count = shifted(
        (slab_p[:e_local], slab_cols[:e_local], slab_count[:e_local]), "rows", -1
    )
    wide_p = jnp.concatenate([prev_p, slab_p, next_p], axis=0)
    wide_cols = jnp.concatenate([prev_cols, slab_cols, next_cols], axis=0)
    wide_count = jnp.concatenate([prev_count, slab_count, next_count], axis=0)
    base_row = row_index * slab_len - e_local
    local_near = neighbours - base_row
    near_p = jnp.take(wide_p, local_near, axis=0)
    near_cols = jnp.take(wide_cols, local_near, axis=0)
    near_live = (
        jnp.arange(p_slot, dtype=jnp.int32)[None, None, :]
        < jnp.take(wide_count, local_near, axis=0)[:, :, None]
    )
    slot_live = jnp.arange(n_slot, dtype=jnp.int32)[None, :] < neighbour_count[:, None]
    own_live = jnp.arange(p_slot, dtype=jnp.int32)[None, :] < p_count[:, None]
    products = jnp.einsum("ekab,ekjbc->ekjac", a_blocks, near_p, precision=HIGH)
    targets = jnp.take(coarse_pattern, p_columns, axis=0)
    select = (
        slot_live[:, None, None, :, None]
        & own_live[:, :, None, None, None]
        & near_live[:, None, None, :, :]
        & (near_cols[:, None, None, :, :] == targets[:, :, :, None, None])
    ).astype(jnp.float32)
    summed = jnp.einsum("ejskl,eklac->ejsac", select, products, precision=HIGH)
    terms = jnp.einsum("ejba,ejsbc->ejsac", p_blocks, summed, precision=HIGH)
    slab_offset = p_columns // agg_slab - row_index + 1
    position = slab_offset * agg_slab + jnp.take(coarse_slot, p_columns, axis=0)
    onehot = (
        position[:, :, None] == jnp.arange(3 * agg_slab, dtype=jnp.int32)[None, None, :]
    ).astype(jnp.float32)
    partial_value = jnp.einsum("ejt,ejsac->tsac", onehot, terms, precision=HIGH)
    from_next = shifted(partial_value[:agg_slab], "rows", -1)
    from_prev = shifted(partial_value[2 * agg_slab :], "rows", 1)
    mine = partial_value[agg_slab : 2 * agg_slab] + from_next + from_prev
    result = lax.psum_scatter(mine, "grp", scatter_dimension=0, tiled=True)
    return result


def solution(mesh):
    return jax.shard_map(
        per_device,
        mesh=mesh,
        in_specs=(
            P(("rows", "grp"), None, None, None),
            P(("rows", "grp"), None),
            P(("rows", "grp")),
            P(("rows", "grp"), None, None, None),
            P(("rows", "grp"), None),
            P(("rows", "grp")),
            P(),
            P(),
        ),
        out_specs=P(("rows", "grp"), None, None, None),
        check_vma=False,
    )
```

profile of v0, /device:TPU:6, one launch (start us, length us, event | category | flops | bytes accessed | tf_op | source)
XLA Modules:
  0.0 224.0 jit_solution(18238891672641204664)
XLA Ops:
  7.3 1.3 dynamic-slice
  9.3 0.9 dynamic-update-slice
  10.1 9.0 %all-reduce = s32[32]{0:T(128)S(1)} all-reduce(s32[32]{0:T(128)S(1)} %dynamic-update-slice), channel_id=1, replica_groups=mesh['rows'=128,'grp'=4] {'grp'}, use_global_device_ids=true, to_apply=%add | all-reduce | flops 32 | bytes 256
  19.2 1.9 collective-permute-start
  21.1 9.1 %collective-permute-start.1 = (s32[8]{0:T(128)S(1)}, s32[8]{0:T(128)S(1)}, u32[]{:S(2)}, u32[]{:S(2)}) collective-permute-start(s32[8]{0:T(128)S(1)} %get-tuple-element.14), channel_id=1, source_target_pairs={{4,0},{8,4},{12,8},{16,12},{20,16},{24,20},{28,24},{32,28},{36,32}... | collective-permute-start | bytes 104 | tf_op jit(solution)/shard_map/ppermute | solution.py:12
  30.2 8.4 %all-gather = s32[4,8,2]{1,2,0:T(2,128)S(1)} all-gather(s32[1,8,2]{1,2,0:T(2,128)} %bitcast.50), channel_id=1, replica_groups=mesh['rows'=128,'grp'=4] {'grp'}, dimensions={0}, use_global_device_ids=true | all-gather | bytes 320 | tf_op jit(solution)/shard_map/all_gather | solution.py:27
  38.7 1.9 collective-permute-start.2
  40.6 5.8 %collective-permute-start.3 = (s32[8,2]{0,1:T(2,128)S(1)}, s32[8,2]{0,1:T(2,128)S(1)}, u32[]{:S(2)}, u32[]{:S(2)}) collective-permute-start(s32[8,2]{0,1:T(2,128)S(1)} %get-tuple-element.12), channel_id=1, source_target_pairs={{4,0},{8,4},{12,8},{16,12},{20,16},{24,20},{28,24},{32,28},{36,32}... | collective-permute-start | bytes 200 | tf_op jit(solution)/shard_map/ppermute | solution.py:12
  46.4 0.8 copy.39
  48.1 0.8 copy.50
  50.7 19.1 %all-gather.3.cloned.1.call-done = f32[32,2,128,128]{3,2,1,0:T(8,128)} async-done(((f32[8,2,128,128]{3,2,1,0:T(8,128)}), f32[32,2,128,128]{3,2,1,0:T(8,128)}) %all-gather.3.cloned.1.call-update) | async-done | bytes 4194320 | tf_op jit(solution)/shard_map/all_gather | solution.py:26
  69.8 2.7 %fusion.34 = (f32[8,2,128,128]{3,2,1,0:T(8,128)}, f32[8,2,128,128]{3,2,1,0:T(8,128)S(1)}) fusion(f32[32,2,128,128]{3,2,1,0:T(8,128)} %all-gather.3.cloned.1.call-done), kind=kLoop, calls=%fused_computation.60 | loop fusion | bytes 4194304 | tf_op jit(solution)/shard_map/slice | solution.py:32
  72.5 1.9 collective-permute-start.4
  74.4 5.8 %collective-permute-start.5 = (f32[8,2,128,128]{3,2,1,0:T(8,128)S(1)}, f32[8,2,128,128]{3,2,1,0:T(8,128)S(1)}, u32[]{:S(2)}, u32[]{:S(2)}) collective-permute-start(f32[8,2,128,128]{3,2,1,0:T(8,128)S(1)} %get-tuple-element.10), channel_id=1, source_target_pairs={{4,0},{8,4},{12,8},{16,12},{20,16},{24,20},{28,24},{32,28},{36,32}... | collective-permute-start | bytes 3145736 | tf_op jit(solution)/shard_map/ppermute | solution.py:12
  80.3 0.8 gather_fusion.1
  82.1 8.8 %collective-permute-done.4 = f32[8,2,128,128]{3,2,1,0:T(8,128)S(1)} collective-permute-done((f32[8,2,128,128]{3,2,1,0:T(8,128)}, f32[8,2,128,128]{3,2,1,0:T(8,128)S(1)}, u32[]{:S(2)}, u32[]{:S(2)}) %collective-permute-start.4) | collective-permute-done | bytes 1048608 | tf_op jit(solution)/shard_map/ppermute | solution.py:12
  90.9 1.6 collective-permute-done.5
  92.5 5.9 %pad_maximum_fusion = f32[48,2,128,128]{3,2,1,0:T(8,128)} fusion(f32[8,2,128,128]{3,2,1,0:T(8,128)S(1)} %collective-permute-done.5, f32[32,2,128,128]{3,2,1,0:T(8,128)} %all-gather.3.cloned.1.call-done, f32[8,2,128,128]{3,2,1,0:T(8,128)S(1)} %collective-permute-done.4), kind=kLoop, calls=%fused_computation.7 | loop fusion | flops 3145728 | bytes 12582912 | tf_op jit(solution)/shard_map/concatenate | solution.py:42
  98.4 6.7 %gather_fusion.4 = f32[56,2,128,128]{3,2,1,0:T(8,128)} fusion(f32[48,2,128,128]{3,2,1,0:T(8,128)} %pad_maximum_fusion, s32[1024]{0:T(1024)S(1)} %pad_clamp_fusion), kind=kCustom, calls=%fused_computation.4 | custom fusion | bytes 14680288 | tf_op jit(solution)/shard_map/jit(_take)/gather | solution.py:47
  105.1 8.5 %copy.51 = f32[8,7,2,128,128]{3,4,2,1,0:T(8,128)} copy(f32[8,7,2,128,128]{4,3,2,1,0:T(8,128)} %bitcast.48) | data formatting | bytes 14680064 | tf_op jit(solution)/shard_map/jit(_take)/gather | solution.py:47
  113.6 11.4 %fusion.7 = f32[8,7,2,128,128,1]{3,4,2,1,0,5:T(8,128)} fusion(f32[8,7,128,128]{3,2,1,0:T(8,128)} %param.8, f32[8,7,2,128,128]{3,4,2,1,0:T(8,128)} %copy.51, pred[8,7]{1,0:T(8,128)(4,1)S(1)} %get-tuple-element.6), kind=kOutput, calls=%fused_computation.13 | convolution fusion | flops 2820407296 | bytes 18350136 | tf_op jit(solution)/shard_map/ekab,ekjbc->ekjac/dot_general | solution.py:55
  125.1 8.9 %copy.58 = f32[8,7,2,128,128,1]{4,1,2,3,5,0:T(8,128)} copy(f32[8,7,2,128,128,1]{3,4,2,1,0,5:T(8,128)} %fusion.7) | data formatting | bytes 14680064 | tf_op jit(solution)/shard_map/ekab,ekjbc->ekjac/transpose | solution.py:55
  133.9 9.9 %convolution_bitcast_fusion.1 = f32[8,2,4,128,128]{4,2,3,1,0:T(4,128)S(1)} fusion(f32[8,7,2,128,128,1]{4,1,2,3,5,0:T(8,128)} %copy.58, s32[8,2,4]{2,1,0:T(2,128)S(1)} %broadcast_select_fusion, s32[8,7,2]{1,2,0:T(2,128)S(1)} %copy.49, pred[8,2,7,2]{2,3,1,0:T(4,128)(4,1)S(1)} %broadcast_and_fusion), kind=kOutput, calls=%fused_computation.15 | convolution fusion | flops 176162560 | bytes 11535264 | tf_op jit(solution)/shard_map/ejskl,eklac->ejsac/dot_general | solution.py:63
  143.9 8.4 %fusion.12 = f32[8,2,4,128,128]{3,4,2,1,0:T(8,128)} fusion(f32[8,2,4,128,128]{4,2,3,1,0:T(4,128)S(1)} %convolution_bitcast_fusion.1, f32[8,2,128,128]{3,2,1,0:T(8,128)S(1)} %copy-done.2), kind=kOutput, calls=%fused_computation.16 | convolution fusion | flops 1610612736 | bytes 9437184 | tf_op jit(solution)/shard_map/ejba,ejsbc->ejsac/dot_general | solution.py:64
  152.3 5.5 %copy.54 = f32[8,2,4,128,128]{4,0,1,3,2:T(8,128)} copy(f32[8,2,4,128,128]{3,4,2,1,0:T(8,128)} %fusion.12) | data formatting | bytes 8388608 | tf_op jit(solution)/shard_map/ejba,ejsbc->ejsac/transpose | solution.py:64
  157.9 4.0 %convolution_bitcast_fusion = f32[12,4,128,128]{3,0,2,1:T(8,128)S(1)} fusion(f32[8,2,4,128,128]{4,0,1,3,2:T(8,128)} %copy.54, s32[8,2]{0,1:T(2,128)S(1)} %copy.45), kind=kOutput, calls=%fused_computation.14 | convolution fusion | flops 150995136 | bytes 7340096 | tf_op jit(solution)/shard_map/ejt,ejsac->tsac/dot_general | solution.py:70
  162.2 5.9 %collective-permute-start.6 = (f32[4,4,128,128]{3,0,2,1:T(4,128)S(1)}, f32[4,4,128,128]{3,0,2,1:T(4,128)S(1)}, u32[]{:S(2)}, u32[]{:S(2)}) collective-permute-start(f32[4,4,128,128]{3,0,2,1:T(4,128)S(1)} %get-tuple-element.7), channel_id=1, source_target_pairs={{4,0},{8,4},{12,8},{16,12},{20,16},{24,20},{28,24},{32,28},{36,32}... | collective-permute-start | bytes 3145736 | tf_op jit(solution)/shard_map/ppermute | solution.py:12
  168.1 1.9 collective-permute-start.7
  170.0 10.4 %collective-permute-done.6 = f32[4,4,128,128]{3,0,2,1:T(4,128)S(1)} collective-permute-done((f32[4,4,128,128]{3,0,2,1:T(4,128)S(1)}, f32[4,4,128,128]{3,0,2,1:T(4,128)S(1)}, u32[]{:S(2)}, u32[]{:S(2)}) %collective-permute-start.6) | collective-permute-done | bytes 1048608 | tf_op jit(solution)/shard_map/ppermute | solution.py:12
  180.4 5.9 %collective-permute-done.7 = f32[4,4,128,128]{3,0,2,1:T(4,128)S(1)} collective-permute-done((f32[4,4,128,128]{3,0,2,1:T(4,128)S(1)}, f32[4,4,128,128]{3,0,2,1:T(4,128)S(1)}, u32[]{:S(2)}, u32[]{:S(2)}) %collective-permute-start.7) | collective-permute-done | bytes 1048608 | tf_op jit(solution)/shard_map/ppermute | solution.py:12
  186.8 1.1 copy.55
  187.9 29.3 %reduce-scatter.2.cloned.1.call-done = f32[1,4,128,128]{3,2,1,0:T(8,128)} async-done(((f32[4,4,128,128]{3,2,1,0:T(8,128)}), f32[1,4,128,128]{3,2,1,0:T(8,128)}) %reduce-scatter.2.cloned.1.call-update) | async-done | bytes 262160 | tf_op jit(solution)/shard_map/reduce_scatter | solution.py:74
  (55 shorter events, 5.4 us)
Async XLA Ops:
  6.5 43.0 %copy-start = (s32[512]{0:T(512)S(1)}, s32[512]{0:T(512)}, u32[]{:S(2)}) copy-start(s32[512]{0:T(512)} %param.14) | copy-start | bytes 6148
  6.5 43.8 %copy-start.4 = (s32[8]{0:T(128)S(1)}, s32[8]{0:T(128)}, u32[]{:S(2)}) copy-start(s32[8]{0:T(128)} %param.13) | copy-start | bytes 100
  6.5 43.9 %copy-start.5 = (s32[8]{0:T(128)S(1)}, s32[8]{0:T(128)}, u32[]{:S(2)}) copy-start(s32[8]{0:T(128)} %param.10) | copy-start | bytes 100
  6.5 63.3 %all-gather.3.cloned.1.call-start = ((), (), s32[]{:S(2)}) async-start(), calls=%async_computation.1 | async-start | bytes 5242880 | tf_op jit(solution)/shard_map/all_gather | solution.py:26
  7.3 209.9 %reduce-scatter.2.cloned.1.call-start = ((), (), s32[]{:S(2)}) async-start(), calls=%async_computation.2 | async-start | bytes 1310720 | tf_op jit(solution)/shard_map/reduce_scatter | solution.py:74
  19.2 55.2 %collective-permute-start = (s32[8]{0:T(128)S(1)}, s32[8]{0:T(128)S(1)}, u32[]{:S(2)}, u32[]{:S(2)}) collective-permute-start(s32[8]{0:T(128)S(1)} %get-tuple-element.13), channel_id=1, source_target_pairs={{0,4},{4,8},{8,12},{12,16},{16,20},{20,24},{24,28},{28,32},{32,36}... | collective-permute-start | bytes 104 | tf_op jit(solution)/shard_map/ppermute | solution.py:12
  21.1 59.0 %collective-permute-start.1 = (s32[8]{0:T(128)S(1)}, s32[8]{0:T(128)S(1)}, u32[]{:S(2)}, u32[]{:S(2)}) collective-permute-start(s32[8]{0:T(128)S(1)} %get-tuple-element.14), channel_id=1, source_target_pairs={{4,0},{8,4},{12,8},{16,12},{20,16},{24,20},{28,24},{32,28},{36,32}... | collective-permute-start | bytes 104 | tf_op jit(solution)/shard_map/ppermute | solution.py:12
  38.7 42.5 %collective-permute-start.2 = (s32[8,2]{0,1:T(2,128)S(1)}, s32[8,2]{0,1:T(2,128)S(1)}, u32[]{:S(2)}, u32[]{:S(2)}) collective-permute-start(s32[8,2]{0,1:T(2,128)S(1)} %get-tuple-element.11), channel_id=1, source_target_pairs={{0,4},{4,8},{8,12},{12,16},{16,20},{20,24},{24,28},{28,32},{32,36}... | collective-permute-start | bytes 200 | tf_op jit(solution)/shard_map/ppermute | solution.py:12
  40.6 40.6 %collective-permute-start.3 = (s32[8,2]{0,1:T(2,128)S(1)}, s32[8,2]{0,1:T(2,128)S(1)}, u32[]{:S(2)}, u32[]{:S(2)}) collective-permute-start(s32[8,2]{0,1:T(2,128)S(1)} %get-tuple-element.12), channel_id=1, source_target_pairs={{4,0},{8,4},{12,8},{16,12},{20,16},{24,20},{28,24},{32,28},{36,32}... | collective-permute-start | bytes 200 | tf_op jit(solution)/shard_map/ppermute | solution.py:12
  50.7 30.4 %copy-start.3 = (s32[8,7]{1,0:T(8,128)S(1)}, s32[8,7]{1,0:T(8,128)}, u32[]{:S(2)}) copy-start(s32[8,7]{1,0:T(8,128)} %param.9) | copy-start | bytes 676
  72.5 18.4 %collective-permute-start.4 = (f32[8,2,128,128]{3,2,1,0:T(8,128)}, f32[8,2,128,128]{3,2,1,0:T(8,128)S(1)}, u32[]{:S(2)}, u32[]{:S(2)}) collective-permute-start(f32[8,2,128,128]{3,2,1,0:T(8,128)} %get-tuple-element.9), channel_id=1, source_target_pairs={{0,4},{4,8},{8,12},{12,16},{16,20},{20,24},{24,28},{28,32},{32,36}... | collective-permute-start | bytes 3145736 | tf_op jit(solution)/shard_map/ppermute | solution.py:12
  74.4 18.1 %collective-permute-start.5 = (f32[8,2,128,128]{3,2,1,0:T(8,128)S(1)}, f32[8,2,128,128]{3,2,1,0:T(8,128)S(1)}, u32[]{:S(2)}, u32[]{:S(2)}) collective-permute-start(f32[8,2,128,128]{3,2,1,0:T(8,128)S(1)} %get-tuple-element.10), channel_id=1, source_target_pairs={{4,0},{8,4},{12,8},{16,12},{20,16},{24,20},{28,24},{32,28},{36,32}... | collective-permute-start | bytes 3145736 | tf_op jit(solution)/shard_map/ppermute | solution.py:12
  133.9 10.0 %copy-start.2 = (f32[8,2,128,128]{3,2,1,0:T(8,128)S(1)}, f32[8,2,128,128]{3,2,1,0:T(8,128)}, u32[]{:S(2)}) copy-start(f32[8,2,128,128]{3,2,1,0:T(8,128)} %param.11) | copy-start | bytes 3145732
  161.9 55.4 %copy-start.1 = (s32[512]{0:T(512)S(1)}, s32[512]{0:T(512)}, u32[]{:S(2)}) copy-start(s32[512]{0:T(512)} %param.14) | copy-start | bytes 6148
  162.2 18.2 %collective-permute-start.6 = (f32[4,4,128,128]{3,0,2,1:T(4,128)S(1)}, f32[4,4,128,128]{3,0,2,1:T(4,128)S(1)}, u32[]{:S(2)}, u32[]{:S(2)}) collective-permute-start(f32[4,4,128,128]{3,0,2,1:T(4,128)S(1)} %get-tuple-element.7), channel_id=1, source_target_pairs={{4,0},{8,4},{12,8},{16,12},{20,16},{24,20},{28,24},{32,28},{36,32}... | collective-permute-start | bytes 3145736 | tf_op jit(solution)/shard_map/ppermute | solution.py:12
  168.1 18.2 %collective-permute-start.7 = (f32[4,4,128,128]{3,0,2,1:T(4,128)S(1)}, f32[4,4,128,128]{3,0,2,1:T(4,128)S(1)}, u32[]{:S(2)}, u32[]{:S(2)}) collective-permute-start(f32[4,4,128,128]{3,0,2,1:T(4,128)S(1)} %get-tuple-element.8), channel_id=1, source_target_pairs={{0,4},{4,8},{8,12},{12,16},{16,20},{20,24},{24,28},{28,32},{32,36}... | collective-permute-start | bytes 3145736 | tf_op jit(solution)/shard_map/ppermute | solution.py:12
Sparse Core Ops, SparseCore 0:
  9.4 60.3 all-gather.2
  188.0 29.1 reduce-scatter.1
where the time goes:
time: 225 us; the launch traced here: 224 us
  waiting for transfers between devices  75.8 us (34%)
  local copies, waits for them, and re-layouts  40.8 us (18%)
  starting transfers between devices  34.2 us (15%)
  matrix products  33.8 us (15%)
  blocking collectives  17.5 us (8%)
  between operations  14.3 us (6%)
  other arithmetic  7.63 us (3%)
    ppermute x8, starting transfers between devices, shifted(): lax.ppermute(value, axis, [(source, source + steps) for source in range(i...  34.2 us
    reduce_scatter x1, waiting for transfers between devices, per_device(): result = lax.psum_scatter(mine, 'grp', scatter_dimension=0, tiled=True)  29.3 us
    ppermute x8, waiting for transfers between devices, shifted(): lax.ppermute(value, axis, [(source, source + steps) for source in range(i...  26.6 us
    all_gather x1, waiting for transfers between devices, per_device(): lax.all_gather(p_blocks, 'grp', axis=0, tiled=True)  19.1 us
    gather x2, local copies, waits for them, and re-layouts, per_device(): near_p = jnp.take(wide_p, local_near, axis=0)  15.2 us
    dot_general x1, matrix products, per_device(): products = jnp.einsum('ekab,ekjbc->ekjac', a_blocks, near_p, precision=HIGH)  11.4 us
    dot_general x1, matrix products, per_device(): summed = jnp.einsum('ejskl,eklac->ejsac', select, products, precision=HIGH)  9.94 us
    unnamed x1, blocking collectives  9.05 us
  transfers between devices with their start and end apart: 10, of which 6 were waited for; matrix products, arithmetic and copies ran while one was open for 5% of the time, Pallas kernels for 0%

commit v1 on v0

v1 whole, which is shorter than its diff:
```python
import functools

import jax
import jax.numpy as jnp
from jax import lax
from jax.experimental import pallas as pl
from jax.experimental.pallas import tpu as pltpu
from jax.sharding import PartitionSpec as P

MESH = pl.DeviceIdType.MESH
F32, BF16, I32 = jnp.float32, jnp.bfloat16, jnp.int32
ORDER = ((2, 0), (2, 1), (1, 1), (3, 0), (1, 0), (3, 1), (0, 0), (0, 1))


def split(value):
    high = value.astype(BF16)
    return high, (value - high.astype(F32)).astype(BF16)


def kernel(
    n_rows, a_hbm, near, near_count, p_hbm, cols, count, slot, pattern, out,
    a_f32, a3, p_win, p3, pt3, prod, z3, terms, meta, meta_s,
    to_prev, to_next, from_next, from_prev, own, from_y,
    a_sem, p_sem, m_sem,
    yp_s, yp_r, ym_s, ym_r, zp_s, zp_r, zm_s, zm_r,
    tn_s, tn_r, tp_s, tp_r, ty_s, ty_r,
):
    e_local, n_slot, size = a_hbm.shape[0], a_hbm.shape[1], a_hbm.shape[2]
    half = e_local // 2
    q, g = lax.axis_index("rows"), lax.axis_index("grp")
    up, down, opp = lax.rem(g + 1, 4), lax.rem(g + 3, 4), lax.rem(g + 2, 4)
    has_prev, has_next = q > 0, q < n_rows - 1
    yp, ym = {"grp": up}, {"grp": down}
    zp, zm = {"rows": q + 1}, {"rows": q - 1}

    def copy(src, dst, ssem, rsem, dev):
        return pltpu.make_async_remote_copy(
            src_ref=src, dst_ref=dst, send_sem=ssem, recv_sem=rsem,
            device_id=dev, device_id_type=MESH,
        )

    own_copy = pltpu.make_async_copy(
        p_hbm, p_win.at[pl.ds(e_local + e_local * g, e_local)], p_sem.at[0]
    )
    own_copy.start()
    a_copies = [
        pltpu.make_async_copy(a_hbm.at[e], a_f32.at[e], a_sem.at[e])
        for e in range(e_local)
    ]
    for c in a_copies:
        c.start()

    row_id = lax.broadcasted_iota(I32, (8, 128), 0)
    lane_id = lax.broadcasted_iota(I32, (8, 128), 1)
    tile = jnp.zeros((8, 128), I32)
    for e in range(e_local):
        for lane, value in ((0, cols[0, e]), (1, cols[1, e]), (2, count[e])):
            tile = jnp.where((row_id == e) & (lane_id == lane), value, tile)
    meta[1 + g] = tile

    @pl.when(q == 0)
    def _():
        meta[0] = jnp.zeros((8, 128), I32)
        for i in range(8):
            from_prev[i] = jnp.zeros(from_prev.shape[1:], F32)

    @pl.when(q == n_rows - 1)
    def _():
        meta[5] = jnp.zeros((8, 128), I32)
        for i in range(8):
            from_next[i] = jnp.zeros(from_next.shape[1:], F32)

    barrier = pltpu.get_barrier_semaphore()
    for dev in (yp, ym):
        pl.semaphore_signal(barrier, inc=1, device_id=dev, device_id_type=MESH)

    @pl.when(has_next)
    def _():
        pl.semaphore_signal(barrier, inc=1, device_id=zp, device_id_type=MESH)

    @pl.when(has_prev)
    def _():
        pl.semaphore_signal(barrier, inc=1, device_id=zm, device_id_type=MESH)

    pl.semaphore_wait(barrier, 2 + has_next.astype(I32) + has_prev.astype(I32))

    def place(src_g, e):
        return p_win.at[e_local + e_local * src_g + e]

    def send_yp(i):
        if i < 8:
            src, dst = p_hbm.at[i], place(g, i)
        elif i == 8:
            src = dst = meta.at[1 + g]
        elif i < 13:
            src = dst = place(down, i - 9)
        else:
            src = dst = meta.at[1 + down]
        return copy(src, dst, yp_s.at[i], yp_r.at[i], yp)

    def send_ym(i):
        if i < 8:
            src, dst = p_hbm.at[i], place(g, i)
        elif i == 8:
            src = dst = meta.at[1 + g]
        else:
            src = dst = place(up, half + i - 9)
        return copy(src, dst, ym_s.at[i], ym_r.at[i], ym)

    def send_zp(e):
        if e < 8:
            src, dst = place(3, e), p_win.at[e]
        else:
            src, dst = meta.at[4], meta.at[0]
        return copy(src, dst, zp_s.at[e], zp_r.at[e], zp)

    def send_zm(e):
        if e < 8:
            src, dst = place(0, e), p_win.at[5 * e_local + e]
        else:
            src, dst = meta.at[1], meta.at[5]
        return copy(src, dst, zm_s.at[e], zm_r.at[e], zm)

    def rim(src_g, e):
        @pl.when((src_g == 3) & has_next)
        def _():
            send_zp(e).start()

        @pl.when((src_g == 0) & has_prev)
        def _():
            send_zm(e).start()

    def widen(index):
        for l in range(2):
            high, low = split(p_win[index, l])
            lanes = pl.ds(l * size, size)
            p3[index, pl.ds(0, size), lanes] = high
            p3[index, pl.ds(size, size), lanes] = high
            p3[index, pl.ds(2 * size, size), lanes] = low

    def prepare(e):
        a_copies[e].wait()
        for k in range(n_slot):
            high, low = split(a_f32[e, k])
            a3[e * n_slot + k, :, pl.ds(0, size)] = high
            a3[e * n_slot + k, :, pl.ds(size, size)] = low
            a3[e * n_slot + k, :, pl.ds(2 * size, size)] = high
        for j in range(2):
            high, low = split(p_win[e_local + e_local * g + e, j].T)
            pt3[2 * e + j, :, pl.ds(0, size)] = high
            pt3[2 * e + j, :, pl.ds(size, size)] = low
            pt3[2 * e + j, :, pl.ds(2 * size, size)] = high

    send_yp(8).start()
    send_ym(8).start()
    for i in range(half):
        send_yp(i).start()
        send_ym(half + i).start()
    own_copy.wait()
    for e in range(9):
        rim(g, e)
    send_yp(8).wait_recv()
    send_yp(13).start()
    rim(down, 8)
    send_ym(8).wait_recv()
    rim(up, 8)
    for e in range(e_local):
        widen(e_local + e_local * g + e)
    for i in range(half):
        send_yp(i).wait_recv()
        send_yp(9 + i).start()
        send_yp(half + i).start()
        rim(down, i)
        send_ym(half + i).wait_recv()
        send_ym(9 + i).start()
        send_ym(i).start()
        rim(up, half + i)
        if i == 0:
            send_yp(13).wait_recv()
            rim(opp, 8)
        widen(e_local + e_local * down + i)
        widen(e_local + e_local * up + half + i)
        prepare(2 * i)
        prepare(2 * i + 1)
    for i in range(half):
        send_yp(9 + i).wait_recv()
        rim(opp, i)
        send_ym(9 + i).wait_recv()
        rim(opp, half + i)
        send_yp(half + i).wait_recv()
        rim(down, half + i)
        send_ym(i).wait_recv()
        rim(up, i)
        widen(e_local + e_local * opp + i)
        widen(e_local + e_local * opp + half + i)
        widen(e_local + e_local * down + half + i)
        widen(e_local + e_local * up + i)

    @pl.when(has_prev)
    def _():
        send_zp(8).wait_recv()

    @pl.when(has_next)
    def _():
        send_zm(8).wait_recv()

    meta_copy = pltpu.make_async_copy(meta, meta_s, m_sem.at[0])
    meta_copy.start()
    for e in range(e_local):
        @pl.when(has_prev)
        def _():
            send_zp(e).wait_recv()
            widen(e)

        @pl.when(has_next)
        def _():
            send_zm(e).wait_recv()
            widen(5 * e_local + e)
    meta_copy.wait()

    base = q * (4 * e_local) - e_local

    def element(e, carry):
        columns = []
        live_k = near_count[e]
        for k in range(n_slot):
            n = jnp.clip(near[e, k] - base, 0, 6 * e_local - 1)
            n_hi, n_lo = lax.shift_right_logical(n, 3), n & 7
            live_l = jnp.where(k < live_k, meta_s[n_hi, n_lo, 2], 0)
            for l in range(2):
                columns.append(jnp.where(l < live_l, meta_s[n_hi, n_lo, l], -1))
            prod[k] = jnp.dot(
                a3[e * n_slot + k], p3[n], preferred_element_type=F32
            )
        live_j = count[e]
        for j in range(2):
            c = cols[j, e]
            for s in range(4):
                target = jnp.where(j < live_j, pattern[s, c], -2)
                total = None
                for k in range(n_slot):
                    for l in range(2):
                        match = jnp.where(columns[2 * k + l] == target, 1.0, 0.0)
                        part = prod[k, :, pl.ds(l * size, size)] * match
                        total = part if total is None else total + part
                high, low = split(total)
                lanes = pl.ds(s * size, size)
                z3[j, pl.ds(0, size), lanes] = high
                z3[j, pl.ds(size, size), lanes] = high
                z3[j, pl.ds(2 * size, size), lanes] = low
            term = jnp.dot(pt3[2 * e + j], z3[j], preferred_element_type=F32)
            for s in range(4):
                terms[2 * e + j, s] = term[:, s * size : (s + 1) * size]
        return carry

    lax.fori_loop(0, e_local, element, 0)

    where = []
    for e in range(e_local):
        for j in range(2):
            c = cols[j, e]
            where.append((lax.shift_right_logical(c, 2) - q + 1) * 4 + slot[c])

    def gather_rows(dst, i, first, slots):
        rel, h = ORDER[i]
        target = first + lax.rem(g + rel, 4)
        for s in range(2):
            total = None
            for x in slots:
                match = jnp.where(where[x] == target, 1.0, 0.0)
                part = terms[x, 2 * h + s] * match
                total = part if total is None else total + part
            dst[i, s] = total

    def send_tp(i):
        return copy(to_prev.at[i], from_next.at[i], tp_s.at[i], tp_r.at[i], zm)

    def send_tn(i):
        return copy(to_next.at[i], from_prev.at[i], tn_s.at[i], tn_r.at[i], zp)

    seconds = [2 * e + 1 for e in range(e_local)]
    for i in range(8):
        @pl.when(has_prev)
        def _():
            gather_rows(to_prev, i, 0, seconds)
            send_tp(i).start()

        @pl.when(has_next)
        def _():
            gather_rows(to_next, i, 8, seconds)
            send_tn(i).start()

    for i in range(8):
        gather_rows(own, i, 4, range(2 * e_local))

    def send_y(i):
        return copy(
            own.at[i], from_y.at[i], ty_s.at[i], ty_r.at[i], yp if i in (0, 2, 4) else ym
        )

    for i in range(8):
        @pl.when(has_next)
        def _():
            send_tp(i).wait_recv()

        @pl.when(has_prev)
        def _():
            send_tn(i).wait_recv()

        total = own[i] + (from_next[i] + from_prev[i])
        if i in (4, 5):
            send_y(i - 4).wait_recv()
            total = total + from_y[i - 4]
        own[i] = total
        if i < 6:
            send_y(i).start()
    for i in (3, 2, 4, 5):
        send_y(i).wait_recv()
    for s in range(2):
        out[0, s] = own[6, s] + (from_y[4, s] + from_y[3, s])
        out[0, 2 + s] = own[7, s] + (from_y[2, s] + from_y[5, s])

    for i in range(14):
        send_yp(i).wait_send()
    for i in range(13):
        send_ym(i).wait_send()

    @pl.when(has_next)
    def _():
        for e in range(9):
            send_zp(e).wait_send()
        for i in range(8):
            send_tn(i).wait_send()

    @pl.when(has_prev)
    def _():
        for e in range(9):
            send_zm(e).wait_send()
        for i in range(8):
            send_tp(i).wait_send()

    for i in range(6):
        send_y(i).wait_send()


def per_device(a, near, near_count, p, cols, count, slot, pattern):
    e_local, n_slot, size = a.shape[0], a.shape[1], a.shape[2]
    smem = pl.BlockSpec(memory_space=pltpu.SMEM)
    anywhere = pl.BlockSpec(memory_space=pl.ANY)
    dma = pltpu.SemaphoreType.DMA
    block = (size, size)
    return pl.pallas_call(
        functools.partial(kernel, lax.axis_size("rows")),
        out_shape=jax.ShapeDtypeStruct((1, 4) + block, F32),
        in_specs=[anywhere, smem, smem, anywhere, smem, smem, smem, smem],
        out_specs=pl.BlockSpec(memory_space=pltpu.VMEM),
        scratch_shapes=[
            pltpu.VMEM(a.shape, F32),
            pltpu.VMEM((e_local * n_slot, size, 3 * size), BF16),
            pltpu.VMEM((6 * e_local, 2) + block, F32),
            pltpu.VMEM((6 * e_local, 3 * size, 2 * size), BF16),
            pltpu.VMEM((2 * e_local, size, 3 * size), BF16),
            pltpu.VMEM((n_slot, size, 2 * size), F32),
            pltpu.VMEM((2, 3 * size, 4 * size), BF16),
            pltpu.VMEM((2 * e_local, 4) + block, F32),
            pltpu.VMEM((6, 8, 128), I32),
            pltpu.SMEM((6, 8, 128), I32),
        ]
        + [pltpu.VMEM((8, 2) + block, F32)] * 5
        + [pltpu.VMEM((6, 2) + block, F32)]
        + [dma((e_local,)), dma((1,)), dma((1,))]
        + [dma((14,)), dma((14,)), dma((13,)), dma((13,))]
        + [dma((9,))] * 4
        + [dma((8,))] * 4
        + [dma((6,))] * 2,
        compiler_params=pltpu.CompilerParams(
            collective_id=0, has_side_effects=True, vmem_limit_bytes=56 << 20
        ),
    )(a, near, near_count, p, cols.T, count, slot, pattern.T)


def solution(mesh):
    return jax.shard_map(
        per_device,
        mesh=mesh,
        in_specs=(
            P(("rows", "grp"), None, None, None),
            P(("rows", "grp"), None),
            P(("rows", "grp")),
            P(("rows", "grp"), None, None, None),
            P(("rows", "grp"), None),
            P(("rows", "grp")),
            P(),
            P(),
        ),
        out_specs=P(("rows", "grp"), None, None, None),
        check_vma=False,
    )
```

time: 225 us -> 77.1 us (0.34)
  waiting for transfers between devices: 75.8 us -> 0 us
  Pallas kernels: 0 us -> 75.2 us
  local copies, waits for them, and re-layouts: 40.8 us -> 1.67 us
  starting transfers between devices: 34.2 us -> 0 us
  matrix products: 33.8 us -> 0 us
  blocking collectives: 17.5 us -> 0 us
  between operations: 14.3 us -> 0.01 us
  other arithmetic: 7.63 us -> 0 us
    pallas_call x0 -> x1, Pallas kernels: none -> 75.2 us  [per_device(): pl.pallas_call(functools.partial(kernel, lax.axis_size('rows')), out_shap...]
    ppermute x8 -> x0, starting transfers between devices: 34.2 us -> none  [shifted(): lax.ppermute(value, axis, [(source, source + steps) for source in range(i...]
    dot_general x4 -> x0, matrix products: 33.8 us -> none  [the longest x1 11.4 us: per_device(): products = jnp.einsum('ekab,ekjbc->ekjac', a_blocks, near_p, precision=HIGH)]
    reduce_scatter x1 -> x0, waiting for transfers between devices: 29.3 us -> none  [per_device(): result = lax.psum_scatter(mine, 'grp', scatter_dimension=0, tiled=True)]
    ppermute x8 -> x0, waiting for transfers between devices: 26.6 us -> none  [shifted(): lax.ppermute(value, axis, [(source, source + steps) for source in range(i...]
    all_gather x1 -> x0, waiting for transfers between devices: 19.1 us -> none  [per_device(): lax.all_gather(p_blocks, 'grp', axis=0, tiled=True)]
    gather x10 -> x0, local copies, waits for them, and re-layouts: 18.1 us -> none  [the longest x2 15.2 us: per_device(): near_p = jnp.take(wide_p, local_near, axis=0)]
    transpose x2 -> x0, local copies, waits for them, and re-layouts: 14.4 us -> none  [the longest x1 8.87 us: per_device(): products = jnp.einsum('ekab,ekjbc->ekjac', a_blocks, near_p, precision=HIGH)]
  transfers between devices with their start and end apart: 10 -> 0, of which waited for: 6 -> 0; matrix products, arithmetic and copies ran while one was open for 5% -> 0% of each run, Pallas kernels for 0% -> 0%
where the time goes in v1:
time: 77.1 us; the launch traced here: 76.9 us
  Pallas kernels  75.2 us (98%)
  local copies, waits for them, and re-layouts  1.67 us (2%)
    pallas_call x1, Pallas kernels, per_device(): pl.pallas_call(functools.partial(kernel, lax.axis_size('rows')), out_shap...  75.2 us
    unnamed x1, local copies, waits for them, and re-layouts  1.67 us

profile of v1, /device:TPU:6, one launch (start us, length us, event | category | flops | bytes accessed | tf_op | source)
XLA Modules:
  0.0 76.9 jit_solution(866705923090989614)
XLA Ops:
  0.0 75.2 %shard_map.82 = f32[1,4,128,128]{3,2,1,0:T(8,128)} custom-call(f32[8,7,128,128]{3,2,1,0:T(8,128)} %a_hbm.1, s32[8,7]{1,0:T(8,128)} %near.1, s32[8]{0:T(128)} %near_count.1, f32[8,2,128,128]{3,2,1,0:T(8,128)} %p_hbm.1, s32[2,8]{1,0:T(2,128)} %bitcast.3, s32[8]{0:T(128)} %count.1, s32[512]{0:T(512)} %slot.1, s32[4,512]{1,0:T(4,128)} %bitcast.2), custom_call_target="tpu_custom_call" | custom-call | tf_op jit(solution)/shard_map/pallas_call | solution.py:352
  75.2 1.7 %copy.10 = f32[1,4,128,128]{3,2,1,0:T(8,128)} copy(f32[1,4,128,128]{3,2,1,0:T(8,128)} %shard_map.82) | data formatting | bytes 524288

commit v2 on v1

--- a/solution.py
+++ b/solution.py
@@ -19,7 +19,8 @@
 
 def kernel(
     n_rows, a_hbm, near, near_count, p_hbm, cols, count, slot, pattern, out,
-    a_f32, a3, p_win, p3, pt3, prod, z3, terms, meta, meta_s,
+    a_f32, a3, p_win, p3, pt3, sums_a, sums_b, z_a, z_b, terms, meta, meta_s,
+    n_s, prev_s, last_s,
     to_prev, to_next, from_next, from_prev, own, from_y,
     a_sem, p_sem, m_sem,
     yp_s, yp_r, ym_s, ym_r, zp_s, zp_r, zm_s, zm_r,
@@ -151,12 +152,44 @@
             pt3[2 * e + j, :, pl.ds(size, size)] = low
             pt3[2 * e + j, :, pl.ds(2 * size, size)] = high
 
+    base = q * (4 * e_local) - e_local
+    n_block = 2 * n_slot
+    meta_copy = pltpu.make_async_copy(meta, meta_s, m_sem.at[0])
+
+    def plan(e, carry):
+        columns = []
+        live_k = near_count[e]
+        for k in range(n_slot):
+            n = jnp.clip(near[e, k] - base, 0, 6 * e_local - 1)
+            n_s[e * n_slot + k] = n
+            n_hi, n_lo = lax.shift_right_logical(n, 3), n & 7
+            live_l = jnp.where(k < live_k, meta_s[n_hi, n_lo, 2], 0)
+            for l in range(2):
+                columns.append(jnp.where(l < live_l, meta_s[n_hi, n_lo, l], -1))
+        for x in range(n_block):
+            found = n_block
+            for y in range(x):
+                found = jnp.where(columns[y] == columns[x], y, found)
+            prev_s[e * n_block + x] = jnp.int32(found)
+        live_j = count[e]
+        for j in range(2):
+            c = cols[j, e]
+            for s in range(4):
+                target = jnp.where(j < live_j, pattern[s, c], -2)
+                found = n_block
+                for x in range(n_block):
+                    found = jnp.where(columns[x] == target, x, found)
+                last_s[e * 8 + 4 * j + s] = found
+        return carry
+
     send_yp(8).start()
     send_ym(8).start()
     for i in range(half):
         send_yp(i).start()
         send_ym(half + i).start()
     own_copy.wait()
+    for sums in (sums_a, sums_b):
+        sums[n_block] = jnp.zeros((size, size), F32)
     for e in range(9):
         rim(g, e)
     send_yp(8).wait_recv()
@@ -195,17 +228,20 @@
         widen(e_local + e_local * opp + half + i)
         widen(e_local + e_local * down + half + i)
         widen(e_local + e_local * up + i)
-
-    @pl.when(has_prev)
-    def _():
-        send_zp(8).wait_recv()
-
-    @pl.when(has_next)
-    def _():
-        send_zm(8).wait_recv()
-
-    meta_copy = pltpu.make_async_copy(meta, meta_s, m_sem.at[0])
-    meta_copy.start()
+        if i == 0:
+            @pl.when(has_prev)
+            def _():
+                send_zp(8).wait_recv()
+
+            @pl.when(has_next)
+            def _():
+                send_zm(8).wait_recv()
+
+            meta_copy.start()
+        if i == 1:
+            meta_copy.wait()
+            lax.fori_loop(0, e_local, plan, 0)
+
     for e in range(e_local):
         @pl.when(has_prev)
         def _():
@@ -216,34 +252,18 @@
         def _():
             send_zm(e).wait_recv()
             widen(5 * e_local + e)
-    meta_copy.wait()
-
-    base = q * (4 * e_local) - e_local
-
-    def element(e, carry):
-        columns = []
-        live_k = near_count[e]
+
+    def element(e, sums, z3):
         for k in range(n_slot):
-            n = jnp.clip(near[e, k] - base, 0, 6 * e_local - 1)
-            n_hi, n_lo = lax.shift_right_logical(n, 3), n & 7
-            live_l = jnp.where(k < live_k, meta_s[n_hi, n_lo, 2], 0)
+            d = jnp.dot(
+                a3[e * n_slot + k], p3[n_s[e * n_slot + k]], preferred_element_type=F32
+            )
             for l in range(2):
-                columns.append(jnp.where(l < live_l, meta_s[n_hi, n_lo, l], -1))
-            prod[k] = jnp.dot(
-                a3[e * n_slot + k], p3[n], preferred_element_type=F32
-            )
-        live_j = count[e]
+                x = 2 * k + l
+                sums[x] = d[:, l * size : (l + 1) * size] + sums[prev_s[e * n_block + x]]
         for j in range(2):
-            c = cols[j, e]
             for s in range(4):
-                target = jnp.where(j < live_j, pattern[s, c], -2)
-                total = None
-                for k in range(n_slot):
-                    for l in range(2):
-                        match = jnp.where(columns[2 * k + l] == target, 1.0, 0.0)
-                        part = prod[k, :, pl.ds(l * size, size)] * match
-                        total = part if total is None else total + part
-                high, low = split(total)
+                high, low = split(sums[last_s[e * 8 + 4 * j + s]])
                 lanes = pl.ds(s * size, size)
                 z3[j, pl.ds(0, size), lanes] = high
                 z3[j, pl.ds(size, size), lanes] = high
@@ -251,9 +271,13 @@
             term = jnp.dot(pt3[2 * e + j], z3[j], preferred_element_type=F32)
             for s in range(4):
                 terms[2 * e + j, s] = term[:, s * size : (s + 1) * size]
+
+    def pair(i, carry):
+        element(2 * i, sums_a, z_a)
+        element(2 * i + 1, sums_b, z_b)
         return carry
 
-    lax.fori_loop(0, e_local, element, 0)
+    lax.fori_loop(0, e_local // 2, pair, 0)
 
     where = []
     for e in range(e_local):
@@ -360,11 +384,16 @@
             pltpu.VMEM((6 * e_local, 2) + block, F32),
             pltpu.VMEM((6 * e_local, 3 * size, 2 * size), BF16),
             pltpu.VMEM((2 * e_local, size, 3 * size), BF16),
-            pltpu.VMEM((n_slot, size, 2 * size), F32),
+            pltpu.VMEM((2 * n_slot + 1,) + block, F32),
+            pltpu.VMEM((2 * n_slot + 1,) + block, F32),
+            pltpu.VMEM((2, 3 * size, 4 * size), BF16),
             pltpu.VMEM((2, 3 * size, 4 * size), BF16),
             pltpu.VMEM((2 * e_local, 4) + block, F32),
             pltpu.VMEM((6, 8, 128), I32),
             pltpu.SMEM((6, 8, 128), I32),
+            pltpu.SMEM((e_local * n_slot,), I32),
+            pltpu.SMEM((2 * e_local * n_slot,), I32),
+            pltpu.SMEM((8 * e_local,), I32),
         ]
         + [pltpu.VMEM((8, 2) + block, F32)] * 5
         + [pltpu.VMEM((6, 2) + block, F32)]

time: 77.1 us -> 73.8 us (0.957)
  Pallas kernels: 75.2 us -> 71.9 us
    pallas_call x1, Pallas kernels: 75.2 us -> 71.9 us  [per_device(): pl.pallas_call(functools.partial(kernel, lax.axis_size('rows')), out_shap...]
where the time goes in v2:
time: 73.8 us; the launch traced here: 73.6 us
  Pallas kernels  71.9 us (97%)
  local copies, waits for them, and re-layouts  1.67 us (2%)
    pallas_call x1, Pallas kernels, per_device(): pl.pallas_call(functools.partial(kernel, lax.axis_size('rows')), out_shap...  71.9 us
    unnamed x1, local copies, waits for them, and re-layouts  1.67 us

profile of v2, /device:TPU:6, one launch (start us, length us, event | category | flops | bytes accessed | tf_op | source)
XLA Modules:
  0.0 73.6 jit_solution(3426909053691563279)
XLA Ops:
  0.0 71.9 %shard_map.82 = f32[1,4,128,128]{3,2,1,0:T(8,128)} custom-call(f32[8,7,128,128]{3,2,1,0:T(8,128)} %a_hbm.1, s32[8,7]{1,0:T(8,128)} %near.1, s32[8]{0:T(128)} %near_count.1, f32[8,2,128,128]{3,2,1,0:T(8,128)} %p_hbm.1, s32[2,8]{1,0:T(2,128)} %bitcast.3, s32[8]{0:T(128)} %count.1, s32[512]{0:T(512)} %slot.1, s32[4,512]{1,0:T(4,128)} %bitcast.2), custom_call_target="tpu_custom_call" | custom-call | tf_op jit(solution)/shard_map/pallas_call | solution.py:376
  71.9 1.7 %copy.10 = f32[1,4,128,128]{3,2,1,0:T(8,128)} copy(f32[1,4,128,128]{3,2,1,0:T(8,128)} %shard_map.82) | data formatting | bytes 524288

commit v3 on v2

--- a/solution.py
+++ b/solution.py
@@ -9,7 +9,10 @@
 
 MESH = pl.DeviceIdType.MESH
 F32, BF16, I32 = jnp.float32, jnp.bfloat16, jnp.int32
-ORDER = ((2, 0), (2, 1), (1, 1), (3, 0), (1, 0), (3, 1), (0, 0), (0, 1))
+ORDER = (
+    (2, 0), (2, 2), (2, 1), (2, 3), (1, 2), (3, 0), (1, 3), (3, 1),
+    (1, 0), (3, 2), (1, 1), (3, 3), (0, 0), (0, 1), (0, 2), (0, 3),
+)
 
 
 def split(value):
@@ -18,11 +21,12 @@
 
 
 def kernel(
-    n_rows, a_hbm, near, near_count, p_hbm, cols, count, slot, pattern, out,
-    a_f32, a3, p_win, p3, pt3, sums_a, sums_b, z_a, z_b, terms, meta, meta_s,
+    n_rows, a_hbm, near_hbm, near_count_hbm, p_hbm, cols_hbm, count_hbm, slot_hbm, pattern_hbm, out,
+    near, near_count, cols, count, slot, pattern,
+    a_f32, a3, p_win, p3, pt3, sums_a, sums_b, z_a, z_b, z_first, terms, meta, meta_s,
     n_s, prev_s, last_s,
     to_prev, to_next, from_next, from_prev, own, from_y,
-    a_sem, p_sem, m_sem,
+    a_sem, p_sem, m_sem, i_sem,
     yp_s, yp_r, ym_s, ym_r, zp_s, zp_r, zm_s, zm_r,
     tn_s, tn_r, tp_s, tp_r, ty_s, ty_r,
 ):
@@ -40,17 +44,46 @@
             device_id=dev, device_id_type=MESH,
         )
 
+    barrier = pltpu.get_barrier_semaphore()
+    for dev in (yp, ym):
+        pl.semaphore_signal(barrier, inc=1, device_id=dev, device_id_type=MESH)
+
+    @pl.when(has_next)
+    def _():
+        pl.semaphore_signal(barrier, inc=1, device_id=zp, device_id_type=MESH)
+
+    @pl.when(has_prev)
+    def _():
+        pl.semaphore_signal(barrier, inc=1, device_id=zm, device_id_type=MESH)
+
+    index_copies = [
+        pltpu.make_async_copy(src, dst, i_sem.at[i])
+        for i, (src, dst) in enumerate((
+            (cols_hbm, cols), (count_hbm, count), (near_hbm, near),
+            (near_count_hbm, near_count), (slot_hbm, slot), (pattern_hbm, pattern),
+        ))
+    ]
+    for c in index_copies:
+        c.start()
     own_copy = pltpu.make_async_copy(
         p_hbm, p_win.at[pl.ds(e_local + e_local * g, e_local)], p_sem.at[0]
     )
     own_copy.start()
-    a_copies = [
-        pltpu.make_async_copy(a_hbm.at[e], a_f32.at[e], a_sem.at[e])
-        for e in range(e_local)
-    ]
-    for c in a_copies:
-        c.start()
-
+
+    @pl.when(q == 0)
+    def _():
+        meta[0] = jnp.zeros((8, 128), I32)
+        for i in range(16):
+            from_prev[i] = jnp.zeros(from_prev.shape[1:], F32)
+
+    @pl.when(q == n_rows - 1)
+    def _():
+        meta[5] = jnp.zeros((8, 128), I32)
+        for i in range(16):
+            from_next[i] = jnp.zeros(from_next.shape[1:], F32)
+
+    for c in index_copies:
+        c.wait()
     row_id = lax.broadcasted_iota(I32, (8, 128), 0)
     lane_id = lax.broadcasted_iota(I32, (8, 128), 1)
     tile = jnp.zeros((8, 128), I32)
@@ -59,31 +92,12 @@
             tile = jnp.where((row_id == e) & (lane_id == lane), value, tile)
     meta[1 + g] = tile
 
-    @pl.when(q == 0)
-    def _():
-        meta[0] = jnp.zeros((8, 128), I32)
-        for i in range(8):
-            from_prev[i] = jnp.zeros(from_prev.shape[1:], F32)
-
-    @pl.when(q == n_rows - 1)
-    def _():
-        meta[5] = jnp.zeros((8, 128), I32)
-        for i in range(8):
-            from_next[i] = jnp.zeros(from_next.shape[1:], F32)
-
-    barrier = pltpu.get_barrier_semaphore()
-    for dev in (yp, ym):
-        pl.semaphore_signal(barrier, inc=1, device_id=dev, device_id_type=MESH)
-
-    @pl.when(has_next)
-    def _():
-        pl.semaphore_signal(barrier, inc=1, device_id=zp, device_id_type=MESH)
-
-    @pl.when(has_prev)
-    def _():
-        pl.semaphore_signal(barrier, inc=1, device_id=zm, device_id_type=MESH)
-
     pl.semaphore_wait(barrier, 2 + has_next.astype(I32) + has_prev.astype(I32))
+
+    a_copies = [
+        pltpu.make_async_copy(a_hbm.at[e], a_f32.at[e], a_sem.at[e])
+        for e in range(e_local)
+    ]
 
     def place(src_g, e):
         return p_win.at[e_local + e_local * src_g + e]
@@ -108,28 +122,29 @@
             src = dst = place(up, half + i - 9)
         return copy(src, dst, ym_s.at[i], ym_r.at[i], ym)
 
-    def send_zp(e):
+    def send_zp(e, mine=False):
         if e < 8:
-            src, dst = place(3, e), p_win.at[e]
+            src, dst = (p_hbm.at[e] if mine else place(3, e)), p_win.at[e]
         else:
             src, dst = meta.at[4], meta.at[0]
         return copy(src, dst, zp_s.at[e], zp_r.at[e], zp)
 
-    def send_zm(e):
+    def send_zm(e, mine=False):
         if e < 8:
-            src, dst = place(0, e), p_win.at[5 * e_local + e]
+            src, dst = (p_hbm.at[e] if mine else place(0, e)), p_win.at[5 * e_local + e]
         else:
             src, dst = meta.at[1], meta.at[5]
         return copy(src, dst, zm_s.at[e], zm_r.at[e], zm)
 
     def rim(src_g, e):
+        mine = src_g is g
         @pl.when((src_g == 3) & has_next)
         def _():
-            send_zp(e).start()
+            send_zp(e, mine).start()
 
         @pl.when((src_g == 0) & has_prev)
         def _():
-            send_zm(e).start()
+            send_zm(e, mine).start()
 
     def widen(index):
         for l in range(2):
@@ -187,26 +202,41 @@
     for i in range(half):
         send_yp(i).start()
         send_ym(half + i).start()
-    own_copy.wait()
+    for e in (8, *range(8)):
+        rim(g, e)
+    for c in a_copies:
+        c.start()
+
     for sums in (sums_a, sums_b):
         sums[n_block] = jnp.zeros((size, size), F32)
-    for e in range(9):
-        rim(g, e)
+    own_copy.wait()
+    for e in range(e_local):
+        widen(e_local + e_local * g + e)
     send_yp(8).wait_recv()
     send_yp(13).start()
     rim(down, 8)
     send_ym(8).wait_recv()
     rim(up, 8)
-    for e in range(e_local):
-        widen(e_local + e_local * g + e)
+    edge = lax.rem(q, 2) * 3
+    own_first, down_first, up_first = g == edge, down == edge, up == edge
+
+    def pieces(relayed, mine):
+        @pl.when(own_first)
+        def _():
+            mine.start()
+            relayed.start()
+
+        @pl.when(jnp.logical_not(own_first))
+        def _():
+            relayed.start()
+            mine.start()
+
     for i in range(half):
         send_yp(i).wait_recv()
-        send_yp(9 + i).start()
-        send_yp(half + i).start()
+        pieces(send_yp(9 + i), send_yp(half + i))
         rim(down, i)
         send_ym(half + i).wait_recv()
-        send_ym(9 + i).start()
-        send_ym(i).start()
+        pieces(send_ym(9 + i), send_ym(i))
         rim(up, half + i)
         if i == 0:
             send_yp(13).wait_recv()
@@ -216,14 +246,22 @@
         prepare(2 * i)
         prepare(2 * i + 1)
     for i in range(half):
+        def from_down():
+            send_yp(half + i).wait_recv()
+            rim(down, half + i)
+
+        def from_up():
+            send_ym(i).wait_recv()
+            rim(up, i)
+
+        pl.when(down_first)(from_down)
+        pl.when(up_first)(from_up)
         send_yp(9 + i).wait_recv()
         rim(opp, i)
         send_ym(9 + i).wait_recv()
         rim(opp, half + i)
-        send_yp(half + i).wait_recv()
-        rim(down, half + i)
-        send_ym(i).wait_recv()
-        rim(up, i)
+        pl.when(jnp.logical_not(down_first))(from_down)
+        pl.when(jnp.logical_not(up_first))(from_up)
         widen(e_local + e_local * opp + i)
         widen(e_local + e_local * opp + half + i)
         widen(e_local + e_local * down + half + i)
@@ -262,15 +300,19 @@
                 x = 2 * k + l
                 sums[x] = d[:, l * size : (l + 1) * size] + sums[prev_s[e * n_block + x]]
         for j in range(2):
+            dst = z3 if j else z_first.at[e]
             for s in range(4):
                 high, low = split(sums[last_s[e * 8 + 4 * j + s]])
                 lanes = pl.ds(s * size, size)
-                z3[j, pl.ds(0, size), lanes] = high
-                z3[j, pl.ds(size, size), lanes] = high
-                z3[j, pl.ds(2 * size, size), lanes] = low
-            term = jnp.dot(pt3[2 * e + j], z3[j], preferred_element_type=F32)
-            for s in range(4):
-                terms[2 * e + j, s] = term[:, s * size : (s + 1) * size]
+                dst[pl.ds(0, size), lanes] = high
+                dst[pl.ds(size, size), lanes] = high
+                dst[pl.ds(2 * size, size), lanes] = low
+        finish(2 * e + 1, z3[...])
+
+    def finish(x, z):
+        term = jnp.dot(pt3[x], z, preferred_element_type=F32)
+        for s in range(4):
+            terms[x, s] = term[:, s * size : (s + 1) * size]
 
     def pair(i, carry):
         element(2 * i, sums_a, z_a)
@@ -286,15 +328,14 @@
             where.append((lax.shift_right_logical(c, 2) - q + 1) * 4 + slot[c])
 
     def gather_rows(dst, i, first, slots):
-        rel, h = ORDER[i]
+        rel, s = ORDER[i]
         target = first + lax.rem(g + rel, 4)
-        for s in range(2):
-            total = None
-            for x in slots:
-                match = jnp.where(where[x] == target, 1.0, 0.0)
-                part = terms[x, 2 * h + s] * match
-                total = part if total is None else total + part
-            dst[i, s] = total
+        total = None
+        for x in slots:
+            match = jnp.where(where[x] == target, 1.0, 0.0)
+            part = terms[x, s] * match
+            total = part if total is None else total + part
+        dst[i] = total
 
     def send_tp(i):
         return copy(to_prev.at[i], from_next.at[i], tp_s.at[i], tp_r.at[i], zm)
@@ -303,7 +344,7 @@
         return copy(to_next.at[i], from_prev.at[i], tn_s.at[i], tn_r.at[i], zp)
 
     seconds = [2 * e + 1 for e in range(e_local)]
-    for i in range(8):
+    for i in range(16):
         @pl.when(has_prev)
         def _():
             gather_rows(to_prev, i, 0, seconds)
@@ -314,15 +355,20 @@
             gather_rows(to_next, i, 8, seconds)
             send_tn(i).start()
 
-    for i in range(8):
-        gather_rows(own, i, 4, range(2 * e_local))
+    def first_slot(e, carry):
+        finish(2 * e, z_first[e])
+        return carry
+
+    lax.fori_loop(0, e_local, first_slot, 0)
 
     def send_y(i):
         return copy(
-            own.at[i], from_y.at[i], ty_s.at[i], ty_r.at[i], yp if i in (0, 2, 4) else ym
+            own.at[i], from_y.at[i], ty_s.at[i], ty_r.at[i], ym if i % 2 else yp
         )
 
-    for i in range(8):
+    for i in range(16):
+        gather_rows(own, i, 4, range(2 * e_local))
+
         @pl.when(has_next)
         def _():
             send_tp(i).wait_recv()
@@ -332,17 +378,16 @@
             send_tn(i).wait_recv()
 
         total = own[i] + (from_next[i] + from_prev[i])
-        if i in (4, 5):
-            send_y(i - 4).wait_recv()
-            total = total + from_y[i - 4]
+        if 8 <= i < 12:
+            send_y(i - 8).wait_recv()
+            total = total + from_y[i - 8]
         own[i] = total
-        if i < 6:
+        if i < 12:
             send_y(i).start()
-    for i in (3, 2, 4, 5):
+    for i in range(4, 12):
         send_y(i).wait_recv()
-    for s in range(2):
-        out[0, s] = own[6, s] + (from_y[4, s] + from_y[3, s])
-        out[0, 2 + s] = own[7, s] + (from_y[2, s] + from_y[5, s])
+    for s, parts in enumerate(((8, 5), (10, 7), (4, 9), (6, 11))):
+        out[0, s] = own[12 + s] + (from_y[parts[0]] + from_y[parts[1]])
 
     for i in range(14):
         send_yp(i).wait_send()
@@ -353,32 +398,35 @@
     def _():
         for e in range(9):
             send_zp(e).wait_send()
-        for i in range(8):
+        for i in range(16):
             send_tn(i).wait_send()
 
     @pl.when(has_prev)
     def _():
         for e in range(9):
             send_zm(e).wait_send()
-        for i in range(8):
+        for i in range(16):
             send_tp(i).wait_send()
 
-    for i in range(6):
+    for i in range(12):
         send_y(i).wait_send()
 
 
 def per_device(a, near, near_count, p, cols, count, slot, pattern):
     e_local, n_slot, size = a.shape[0], a.shape[1], a.shape[2]
-    smem = pl.BlockSpec(memory_space=pltpu.SMEM)
     anywhere = pl.BlockSpec(memory_space=pl.ANY)
     dma = pltpu.SemaphoreType.DMA
     block = (size, size)
     return pl.pallas_call(
         functools.partial(kernel, lax.axis_size("rows")),
-        out_shape=jax.ShapeDtypeStruct((1, 4) + block, F32),
-        in_specs=[anywhere, smem, smem, anywhere, smem, smem, smem, smem],
+        out_shape=pltpu.VMEM((1, 4) + block, F32),
+        in_specs=[anywhere] * 8,
         out_specs=pl.BlockSpec(memory_space=pltpu.VMEM),
         scratch_shapes=[
+            pltpu.SMEM(x.shape, I32)
+            for x in (near, near_count, cols.T, count, slot, pattern.T)
+        ]
+        + [
             pltpu.VMEM(a.shape, F32),
             pltpu.VMEM((e_local * n_slot, size, 3 * size), BF16),
             pltpu.VMEM((6 * e_local, 2) + block, F32),
@@ -386,8 +434,9 @@
             pltpu.VMEM((2 * e_local, size, 3 * size), BF16),
             pltpu.VMEM((2 * n_slot + 1,) + block, F32),
             pltpu.VMEM((2 * n_slot + 1,) + block, F32),
-            pltpu.VMEM((2, 3 * size, 4 * size), BF16),
-            pltpu.VMEM((2, 3 * size, 4 * size), BF16),
+            pltpu.VMEM((3 * size, 4 * size), BF16),
+            pltpu.VMEM((3 * size, 4 * size), BF16),
+            pltpu.VMEM((e_local, 3 * size, 4 * size), BF16),
             pltpu.VMEM((2 * e_local, 4) + block, F32),
             pltpu.VMEM((6, 8, 128), I32),
             pltpu.SMEM((6, 8, 128), I32),
@@ -395,13 +444,13 @@
             pltpu.SMEM((2 * e_local * n_slot,), I32),
             pltpu.SMEM((8 * e_local,), I32),
         ]
-        + [pltpu.VMEM((8, 2) + block, F32)] * 5
-        + [pltpu.VMEM((6, 2) + block, F32)]
-        + [dma((e_local,)), dma((1,)), dma((1,))]
+        + [pltpu.VMEM((16,) + block, F32)] * 5
+        + [pltpu.VMEM((12,) + block, F32)]
+        + [dma((e_local,)), dma((1,)), dma((1,)), dma((6,))]
         + [dma((14,)), dma((14,)), dma((13,)), dma((13,))]
         + [dma((9,))] * 4
-        + [dma((8,))] * 4
-        + [dma((6,))] * 2,
+        + [dma((16,))] * 4
+        + [dma((12,))] * 2,
         compiler_params=pltpu.CompilerParams(
             collective_id=0, has_side_effects=True, vmem_limit_bytes=56 << 20
         ),

time: 73.8 us -> 71.6 us (0.970)
  Pallas kernels: 71.9 us -> 70.7 us
  local copies, waits for them, and re-layouts: 1.67 us -> 0.71 us
    pallas_call x1, Pallas kernels: 71.9 us -> 70.7 us  [per_device(): pl.pallas_call(functools.partial(kernel, lax.axis_size('rows')), out_shap...]
    unnamed x1, local copies, waits for them, and re-layouts: 1.67 us -> 0.71 us
where the time goes in v3:
time: 71.6 us; the launch traced here: 71.4 us
  Pallas kernels  70.7 us (99%)
    pallas_call x1, Pallas kernels, per_device(): pl.pallas_call(functools.partial(kernel, lax.axis_size('rows')), out_shap...  70.7 us

profile of v3, /device:TPU:6, one launch (start us, length us, event | category | flops | bytes accessed | tf_op | source)
XLA Modules:
  0.0 71.4 jit_solution(7467720224665181642)
XLA Ops:
  0.0 70.7 %shard_map.82 = f32[1,4,128,128]{3,2,1,0:T(8,128)S(1)} custom-call(f32[8,7,128,128]{3,2,1,0:T(8,128)} %a_hbm.1, s32[8,7]{1,0:T(8,128)} %near_hbm.1, s32[8]{0:T(128)} %near_count_hbm.1, f32[8,2,128,128]{3,2,1,0:T(8,128)} %p_hbm.1, s32[2,8]{1,0:T(2,128)} %bitcast.3, s32[8]{0:T(128)} %count_hbm.1, s32[512]{0:T(512)} %slot_hbm.1, s32[4,512]{1,0:T(4,128)} %bitcast.2), custom_call_target="tpu_custom_call" | custom-call | tf_op jit(solution)/shard_map/pallas_call | solution.py:420
  70.7 0.7 copy.10

commit v4 on v3

--- a/solution.py
+++ b/solution.py
@@ -24,7 +24,7 @@
     n_rows, a_hbm, near_hbm, near_count_hbm, p_hbm, cols_hbm, count_hbm, slot_hbm, pattern_hbm, out,
     near, near_count, cols, count, slot, pattern,
     a_f32, a3, p_win, p3, pt3, sums_a, sums_b, z_a, z_b, z_first, terms, meta, meta_s,
-    n_s, prev_s, last_s,
+    n_s, prev_s, last_s, first,
     to_prev, to_next, from_next, from_prev, own, from_y,
     a_sem, p_sem, m_sem, i_sem,
     yp_s, yp_r, ym_s, ym_r, zp_s, zp_r, zm_s, zm_r,
@@ -161,6 +161,9 @@
             a3[e * n_slot + k, :, pl.ds(0, size)] = high
             a3[e * n_slot + k, :, pl.ds(size, size)] = low
             a3[e * n_slot + k, :, pl.ds(2 * size, size)] = high
+        first[e] = jnp.dot(
+            a3[e * n_slot], p3[e_local + e_local * g + e], preferred_element_type=F32
+        )
         for j in range(2):
             high, low = split(p_win[e_local + e_local * g + e, j].T)
             pt3[2 * e + j, :, pl.ds(0, size)] = high
@@ -293,7 +296,7 @@
 
     def element(e, sums, z3):
         for k in range(n_slot):
-            d = jnp.dot(
+            d = first[e] if k == 0 else jnp.dot(
                 a3[e * n_slot + k], p3[n_s[e * n_slot + k]], preferred_element_type=F32
             )
             for l in range(2):
@@ -443,6 +446,7 @@
             pltpu.SMEM((e_local * n_slot,), I32),
             pltpu.SMEM((2 * e_local * n_slot,), I32),
             pltpu.SMEM((8 * e_local,), I32),
+            pltpu.VMEM((e_local, size, 2 * size), F32),
         ]
         + [pltpu.VMEM((16,) + block, F32)] * 5
         + [pltpu.VMEM((12,) + block, F32)]

time: 71.6 us -> 71.2 us (level)
  no operation moved by 1% of the time
where the time goes in v4:
time: 71.2 us; the launch traced here: 71 us
  Pallas kernels  70.3 us (99%)
    pallas_call x1, Pallas kernels, per_device(): pl.pallas_call(functools.partial(kernel, lax.axis_size('rows')), out_shap...  70.3 us

profile of v4, /device:TPU:6, one launch (start us, length us, event | category | flops | bytes accessed | tf_op | source)
XLA Modules:
  0.0 71.0 jit_solution(15269602953846916805)
XLA Ops:
  0.0 70.3 %shard_map.82 = f32[1,4,128,128]{3,2,1,0:T(8,128)S(1)} custom-call(f32[8,7,128,128]{3,2,1,0:T(8,128)} %a_hbm.1, s32[8,7]{1,0:T(8,128)} %near_hbm.1, s32[8]{0:T(128)} %near_count_hbm.1, f32[8,2,128,128]{3,2,1,0:T(8,128)} %p_hbm.1, s32[2,8]{1,0:T(2,128)} %bitcast.3, s32[8]{0:T(128)} %count_hbm.1, s32[512]{0:T(512)} %slot_hbm.1, s32[4,512]{1,0:T(4,128)} %bitcast.2), custom_call_target="tpu_custom_call" | custom-call | tf_op jit(solution)/shard_map/pallas_call | solution.py:423
  70.3 0.7 copy.10
